TPU v7x, 128 devices: a whole 4x4x4 slice. The times are simulated.
128 devices in a mesh: row: 16 (over z, y), col: 8 (over x, core).
Axes of the slice: x: 4, y: 4, z: 4, core: 2. Of those that a mesh axis runs over, the one named last changes fastest.
Arguments:
- amplitudes: bfloat16 [16, 4, 1024, 1024], P(None, None, 'row', 'col'), may hold values from -6 to 6
- cycle_integrals: bfloat16 [4, 8, 1024, 1024], P(None, None, 'row', 'col'), may hold values from -0.375 to 0.375
- mask_amp: int32 [16, 16], replicated, may hold values 0 or 1
- mask_int: int32 [16, 16], replicated, may hold values 0 or 1
- occupied_i: float32 [16], P('row'), may hold values from -1 to -0.3
- occupied_j: float32 [8], P('col'), may hold values from -1 to -0.3
- virtual_energy: float32 [1024], replicated, may hold values from 0.2 to 1.5
Outputs:
- update: bfloat16 [16, 8, 1024, 1024], P('row', 'col')
Inputs may be any that keep to these rules, and one draw needn't show every extreme that they name: mask_amp holds 0 or 1: 1 where the amplitude tile survives screening. mask_int holds 0 or 1: 1 where the intermediate tile survives screening.
All inputs are finite; a program needn't handle non-finite values.
Results may differ from a plain program's by a relative error of at most 0.0049.
Values may be sent and summed in bfloat16 or wider, within the bound.
A program may use at most 192 MiB of HBM per device.

v0:
```python
import jax
import jax.numpy as jnp
from jax import lax
from jax.sharding import PartitionSpec as P

TILE = 64


def local_mask(mask, row_first, row_tiles, col_first, col_tiles):
    window = lax.dynamic_slice(mask, (row_first, col_first), (row_tiles, col_tiles))
    return jnp.repeat(jnp.repeat(window, TILE, axis=0), TILE, axis=1).astype(jnp.bfloat16)


def per_device(
    amplitudes, cycle_integrals, mask_amp, mask_int, occupied_i, occupied_j, virtual_energy
):
    row_index = lax.axis_index("row")
    col_index = lax.axis_index("col")
    row_tiles = amplitudes.shape[2] // TILE
    col_tiles = amplitudes.shape[3] // TILE
    amp_masked = (
        amplitudes
        * local_mask(mask_amp, row_index * row_tiles, row_tiles, col_index * col_tiles, col_tiles)[
            None, None
        ]
    )
    int_masked = (
        cycle_integrals
        * local_mask(mask_int, row_index * row_tiles, row_tiles, col_index * col_tiles, col_tiles)[
            None, None
        ]
    )
    whole = virtual_energy.shape[0]
    partial_value = jnp.einsum(
        "ikac,kjbc->ijab",
        amp_masked,
        lax.all_gather(int_masked, "row", axis=2, tiled=True),
        preferred_element_type=jnp.float32,
    )
    exchanged = lax.all_to_all(
        lax.all_to_all(partial_value[None], "row", split_axis=1, concat_axis=3, tiled=True),
        "col",
        split_axis=2,
        concat_axis=0,
        tiled=True,
    )
    cycle = jnp.sum(exchanged, axis=0).astype(jnp.bfloat16)
    denominator = virtual_energy[:, None] + virtual_energy[None, :] - occupied_i[0] - occupied_j[0]
    result = cycle.reshape(whole, whole).astype(jnp.float32) / denominator
    return result.astype(jnp.bfloat16)[None, None]


def solution(mesh):
    in_specs = (
        P(None, None, "row", "col"),
        P(None, None, "row", "col"),
        P(),
        P(),
        P("row"),
        P("col"),
        P(),
    )
    out_specs = P("row", "col", None, None)
    return jax.shard_map(
        per_device, mesh=mesh, in_specs=in_specs, out_specs=out_specs, check_vma=False
    )
```

profile of v0, /device:TPU:1, one launch (start us, length us, event | category | flops | bytes accessed | tf_op | source)
XLA Modules:
  0.0 901.8 jit_solution(1429564766172475192)
XLA Ops:
  6.5 0.0 all-gather.2.cloned.1.call-start
  6.5 0.8 convert_bitcast_fusion
  7.3 0.1 broadcast_in_dim.6
  7.4 0.1 convert_element_type.63
  7.5 1.9 copy_multiply_fusion
  9.4 0.0 all-gather.2.cloned.1.call-update
  9.4 0.1 broadcast_in_dim.7
  9.4 0.1 convert_element_type.66
  9.5 74.1 %all-gather.2.cloned.1.call-done = bf16[4,8,1024,128]{3,2,0,1:T(8,128)(2,1)} async-done(((bf16[4,8,64,128]{3,2,0,1:T(8,128)(2,1)}), bf16[4,8,1024,128]{3,2,0,1:T(8,128)(2,1)}) %all-gather.2.cloned.1.call-update) | async-done | bytes 8388624 | tf_op jit(solution)/shard_map/all_gather | solution.py:37
  83.6 18.9 %convolution_bitcast_fusion = f32[1,16,8,64,1024]{4,3,1,2,0:T(8,128)} fusion(bf16[4,8,1024,128]{3,2,0,1:T(8,128)(2,1)} %all-gather.2.cloned.1.call-done, bf16[16,4,64,128]{3,2,1,0:T(8,128)(2,1)} %param.7, bf16[128]{0:T(256)(128)(2,1)S(1)} %convert_element_type.66), kind=kOutput, calls=%fused_computation | convolution fusion | flops 8592031744 | bytes 42991872 | tf_op jit(solution)/shard_map/ikac,kjbc->ijab/dot_general | solution.py:34
  102.5 12.1 %copy.12 = f32[1,16,8,64,1024]{4,3,2,0,1:T(8,128)S(1)} copy(f32[1,16,8,64,1024]{4,3,1,2,0:T(8,128)} %convolution_bitcast_fusion) | data formatting | bytes 67108864 | tf_op jit(solution)/shard_map/broadcast_in_dim | solution.py:41
  114.6 369.3 %all_to_all.27 = f32[1,16,8,64,1024]{4,3,2,0,1:T(8,128)} all-to-all(f32[1,16,8,64,1024]{4,3,2,0,1:T(8,128)S(1)} %copy.12), channel_id=1, replica_groups=mesh['row'=16,'col'=8] {'row'}, dimensions={1} | all-to-all | bytes 67108864 | tf_op jit(solution)/shard_map/all_to_all | solution.py:41
  483.9 23.3 %copy.13 = f32[1,16,8,64,1024]{4,3,1,2,0:T(8,128)} copy(f32[1,16,8,64,1024]{4,3,2,0,1:T(8,128)} %all_to_all.27) | data formatting | bytes 67108864 | tf_op jit(solution)/shard_map/all_to_all | solution.py:41
  507.3 9.0 %all-to-all-start.1 = ((f32[1,1,8,1024,1024]{4,3,1,0,2:T(8,128)}), f32[1,1,8,1024,1024]{4,3,1,0,2:T(8,128)}, u32[]{:S(2)}, u32[]{:S(2)}) async-start(f32[1,1,8,1024,1024]{4,3,1,0,2:T(8,128)} %bitcast.33), calls=%async_computation.1 | async-start | bytes 67108864 | tf_op jit(solution)/shard_map/all_to_all | solution.py:40
  517.6 0.0 copy-start
  517.6 362.2 %all-to-all-done.1 = f32[1,1,8,1024,1024]{4,3,1,0,2:T(8,128)} async-done(((f32[1,1,8,1024,1024]{4,3,1,0,2:T(8,128)}), f32[1,1,8,1024,1024]{4,3,1,0,2:T(8,128)}, u32[]{:S(2)}, u32[]{:S(2)}) %all-to-all-start.1) | async-done | bytes 33554464 | tf_op jit(solution)/shard_map/all_to_all | solution.py:40
  879.8 12.9 %reduce_sum.9 = bf16[1024,1024]{1,0:T(8,128)(2,1)S(1)} reduce(f32[1,1,8,1024,1024]{4,3,1,0,2:T(8,128)} %all-to-all-done.1, f32[]{:T(128)} %constant.16.clone.1), dimensions={0,1,2}, to_apply=%region_0.0 | reduce | flops 7340032 | bytes 35651588 | tf_op jit(solution)/shard_map/reduce_sum | solution.py:47
  892.7 0.0 copy-done
  892.7 2.3 fusion.1
Async XLA Ops:
  6.5 77.1 %all-gather.2.cloned.1.call-start = ((), (), s32[]{:S(2)}) async-start(), calls=%async_computation.2 | async-start | bytes 8912896 | tf_op jit(solution)/shard_map/all_gather | solution.py:37
  507.3 372.6 %all-to-all-start.1 = ((f32[1,1,8,1024,1024]{4,3,1,0,2:T(8,128)}), f32[1,1,8,1024,1024]{4,3,1,0,2:T(8,128)}, u32[]{:S(2)}, u32[]{:S(2)}) async-start(f32[1,1,8,1024,1024]{4,3,1,0,2:T(8,128)} %bitcast.33), calls=%async_computation.1 | async-start | bytes 67108864 | tf_op jit(solution)/shard_map/all_to_all | solution.py:40
  517.6 375.1 %copy-start = (f32[1024]{0:T(1024)S(1)}, f32[1024]{0:T(1024)}, u32[]{:S(2)}) copy-start(f32[1024]{0:T(1024)} %param.13) | copy-start | bytes 12292
Sparse Core Ops, SparseCore 0:
  9.5 74.0 all-gather.1
where the time goes:
time: 902 us
  waiting for transfers between devices  436 us (48%)
  blocking collectives  369 us (41%)
  local copies, waits for them, and re-layouts  35.8 us (4%)
  matrix products  18.9 us (2%)
  other arithmetic  17.8 us (2%)
  between operations  14.7 us (2%)
  starting transfers between devices  9.05 us (1%)
    all_to_all x1, blocking collectives, per_device(): lax.all_to_all(partial_value[None], 'row', split_axis=1, concat_axis=3, t...  369 us
    all_to_all x1, waiting for transfers between devices, per_device(): lax.all_to_all(lax.all_to_all(partial_value[None], 'row', split_axis=1, c...  362 us
    all_gather x1, waiting for transfers between devices, per_device(): lax.all_gather(int_masked, 'row', axis=2, tiled=True)  74.1 us
    all_to_all x1, local copies, waits for them, and re-layouts, per_device(): lax.all_to_all(partial_value[None], 'row', split_axis=1, concat_axis=3, t...  23.3 us
    dot_general x1, matrix products, per_device(): jnp.einsum('ikac,kjbc->ijab', amp_masked, lax.all_gather(int_masked, 'row...  18.9 us
  transfers between devices with their start and end apart: 2, of which 2 were waited for; matrix products, arithmetic and copies ran while one was open for 0% of the time, Pallas kernels for 0%

commit v1 on v0

--- a/solution.py
+++ b/solution.py
@@ -34,7 +34,9 @@
     partial_value = jnp.einsum(
         "ikac,kjbc->ijab",
         amp_masked,
-        lax.all_gather(int_masked, "row", axis=2, tiled=True),
+        jnp.concatenate(
+            lax.all_to_all(jnp.stack([int_masked] * lax.axis_size("row")), "row", 0, 0), axis=2
+        ),
         preferred_element_type=jnp.float32,
     )
     exchanged = lax.all_to_all(

time: 902 us -> 966 us (1.071)
  waiting for transfers between devices: 436 us -> 485 us
  local copies, waits for them, and re-layouts: 35.8 us -> 50.8 us
  between operations: 14.7 us -> 1.36 us
  starting transfers between devices: 9.05 us -> 18.8 us
    all_to_all x0 -> x1, waiting for transfers between devices: none -> 123 us  [per_device(): lax.all_to_all(jnp.stack([int_masked] * lax.axis_size('row')), 'row', 0, 0)]
    all_gather x1 -> x0, waiting for transfers between devices: 74.1 us -> none  [per_device(): lax.all_gather(int_masked, 'row', axis=2, tiled=True)]
where the time goes in v1:
time: 966 us; the launch traced here: 965 us
  waiting for transfers between devices  485 us (50%)
  blocking collectives  374 us (39%)
  local copies, waits for them, and re-layouts  50.8 us (5%)
  starting transfers between devices  18.8 us (2%)
  matrix products  18.7 us (2%)
  other arithmetic  17 us (2%)
    all_to_all x1, blocking collectives, per_device(): lax.all_to_all(partial_value[None], 'row', split_axis=1, concat_axis=3, t...  374 us
    all_to_all x1, waiting for transfers between devices, per_device(): lax.all_to_all(lax.all_to_all(partial_value[None], 'row', split_axis=1, c...  362 us
    all_to_all x1, waiting for transfers between devices, per_device(): lax.all_to_all(jnp.stack([int_masked] * lax.axis_size('row')), 'row', 0, 0)  123 us
    all_to_all x1, local copies, waits for them, and re-layouts, per_device(): lax.all_to_all(partial_value[None], 'row', split_axis=1, concat_axis=3, t...  23.3 us
  transfers between devices with their start and end apart: 2, of which 2 were waited for; matrix products, arithmetic and copies ran while one was open for 0% of the time, Pallas kernels for 0%

profile of v1, /device:TPU:1, one launch (start us, length us, event | category | flops | bytes accessed | tf_op | source)
XLA Modules:
  0.0 965.3 jit_solution(559311313463763385)
XLA Ops:
  0.0 0.8 convert_bitcast_fusion
  0.8 0.1 broadcast_in_dim.6
  0.9 0.1 convert_element_type.63
  0.9 1.1 broadcast_multiply_fusion
  2.1 5.4 stack.2
  7.4 8.6 all-to-all-start
  16.1 0.1 broadcast_in_dim.7
  16.2 0.1 convert_element_type.66
  16.2 123.0 %all-to-all-done = bf16[16,4,8,64,128]{4,3,1,2,0:T(8,128)(2,1)} async-done(((bf16[16,4,8,64,128]{4,3,1,2,0:T(8,128)(2,1)}), bf16[16,4,8,64,128]{4,3,1,2,0:T(8,128)(2,1)}, u32[]{:S(2)}, u32[]{:S(2)}) %all-to-all-start) | async-done | bytes 8388640 | tf_op jit(solution)/shard_map/all_to_all | solution.py:38
  139.2 0.0 copy-start.1
  139.2 9.7 %copy.13 = bf16[4,8,16,64,128]{4,3,2,0,1:T(8,128)(2,1)} copy(bf16[4,8,16,64,128]{4,3,0,1,2:T(8,128)(2,1)} %bitcast.1) | data formatting | bytes 16777216 | tf_op jit(solution)/shard_map/reshape | solution.py:37
  148.9 0.0 copy-done.1
  148.9 18.7 %convolution_bitcast_fusion = f32[1,16,8,64,1024]{4,3,1,2,0:T(8,128)} fusion(bf16[4,8,1024,128,1]{3,2,0,4,1:T(8,128)(2,1)} %bitcast.36, bf16[16,4,64,128]{3,2,1,0:T(8,128)(2,1)S(1)} %copy-done.1, bf16[128]{0:T(256)(128)(2,1)S(1)} %convert_element_type.66), kind=kOutput, calls=%fused_computation | convolution fusion | flops 8592031744 | bytes 42991872 | tf_op jit(solution)/shard_map/ikac,kjbc->ijab/dot_general | solution.py:34
  167.6 12.1 %copy.14 = f32[1,16,8,64,1024]{4,3,2,0,1:T(8,128)S(1)} copy(f32[1,16,8,64,1024]{4,3,1,2,0:T(8,128)} %convolution_bitcast_fusion) | data formatting | bytes 67108864 | tf_op jit(solution)/shard_map/broadcast_in_dim | solution.py:43
  179.7 373.5 %all_to_all.32 = f32[1,16,8,64,1024]{4,3,2,0,1:T(8,128)} all-to-all(f32[1,16,8,64,1024]{4,3,2,0,1:T(8,128)S(1)} %copy.14), channel_id=1, replica_groups=mesh['row'=16,'col'=8] {'row'}, dimensions={1} | all-to-all | bytes 67108864 | tf_op jit(solution)/shard_map/all_to_all | solution.py:43
  553.2 23.3 %copy.15 = f32[1,16,8,64,1024]{4,3,1,2,0:T(8,128)} copy(f32[1,16,8,64,1024]{4,3,2,0,1:T(8,128)} %all_to_all.32) | data formatting | bytes 67108864 | tf_op jit(solution)/shard_map/all_to_all | solution.py:43
  576.5 10.1 %all-to-all-start.2 = ((f32[1,1,8,1024,1024]{4,3,1,0,2:T(8,128)}), f32[1,1,8,1024,1024]{4,3,1,0,2:T(8,128)}, u32[]{:S(2)}, u32[]{:S(2)}) async-start(f32[1,1,8,1024,1024]{4,3,1,0,2:T(8,128)} %bitcast.35), calls=%async_computation.2 | async-start | bytes 67108864 | tf_op jit(solution)/shard_map/all_to_all | solution.py:42
  587.9 0.0 copy-start
  588.0 362.2 %all-to-all-done.2 = f32[1,1,8,1024,1024]{4,3,1,0,2:T(8,128)} async-done(((f32[1,1,8,1024,1024]{4,3,1,0,2:T(8,128)}), f32[1,1,8,1024,1024]{4,3,1,0,2:T(8,128)}, u32[]{:S(2)}, u32[]{:S(2)}) %all-to-all-start.2) | async-done | bytes 33554464 | tf_op jit(solution)/shard_map/all_to_all | solution.py:42
  950.2 12.9 %reduce_sum.9 = bf16[1024,1024]{1,0:T(8,128)(2,1)S(1)} reduce(f32[1,1,8,1024,1024]{4,3,1,0,2:T(8,128)} %all-to-all-done.2, f32[]{:T(128)} %constant.16.clone.1), dimensions={0,1,2}, to_apply=%region_0.0 | reduce | flops 7340032 | bytes 35651588 | tf_op jit(solution)/shard_map/reduce_sum | solution.py:49
  963.0 0.0 copy-done
  963.0 2.3 fusion
  (1 shorter events, 0.0 us)
Async XLA Ops:
  7.4 131.8 %all-to-all-start = ((bf16[16,4,8,64,128]{4,3,1,2,0:T(8,128)(2,1)}), bf16[16,4,8,64,128]{4,3,1,2,0:T(8,128)(2,1)}, u32[]{:S(2)}, u32[]{:S(2)}) async-start(bf16[16,4,8,64,128]{4,3,1,2,0:T(8,128)(2,1)} %stack.2), calls=%async_computation | async-start | bytes 16777216 | tf_op jit(solution)/shard_map/all_to_all | solution.py:38
  139.2 9.7 %copy-start.1 = (bf16[16,4,64,128]{3,2,1,0:T(8,128)(2,1)S(1)}, bf16[16,4,64,128]{3,2,1,0:T(8,128)(2,1)}, u32[]{:S(2)}) copy-start(bf16[16,4,64,128]{3,2,1,0:T(8,128)(2,1)} %param.7) | copy-start | bytes 3145732
  576.5 373.7 %all-to-all-start.2 = ((f32[1,1,8,1024,1024]{4,3,1,0,2:T(8,128)}), f32[1,1,8,1024,1024]{4,3,1,0,2:T(8,128)}, u32[]{:S(2)}, u32[]{:S(2)}) async-start(f32[1,1,8,1024,1024]{4,3,1,0,2:T(8,128)} %bitcast.35), calls=%async_computation.2 | async-start | bytes 67108864 | tf_op jit(solution)/shard_map/all_to_all | solution.py:42
  587.9 375.1 %copy-start = (f32[1024]{0:T(1024)S(1)}, f32[1024]{0:T(1024)}, u32[]{:S(2)}) copy-start(f32[1024]{0:T(1024)} %param.13) | copy-start | bytes 12292

commit v2 on v0

--- a/solution.py
+++ b/solution.py
@@ -38,7 +38,12 @@
         preferred_element_type=jnp.float32,
     )
     exchanged = lax.all_to_all(
-        lax.all_to_all(partial_value[None], "row", split_axis=1, concat_axis=3, tiled=True),
+        jnp.concatenate(
+            lax.all_to_all(
+                jnp.stack(jnp.split(partial_value[None], lax.axis_size("row"), axis=1)), "row", 0, 0
+            ),
+            axis=3,
+        ),
         "col",
         split_axis=2,
         concat_axis=0,

time: 902 us -> 929 us (1.030)
  local copies, waits for them, and re-layouts: 35.8 us -> 62 us
    unnamed x2 -> x17, local copies, waits for them, and re-layouts: 0.01 us -> 47.5 us
    all_to_all x1 -> x0, local copies, waits for them, and re-layouts: 23.3 us -> none  [per_device(): lax.all_to_all(partial_value[None], 'row', split_axis=1, concat_axis=3, t...]
    broadcast_in_dim x1 -> x0, local copies, waits for them, and re-layouts: 12.1 us -> none  [per_device(): partial_value[None]]
    reshape x0 -> x1, local copies, waits for them, and re-layouts: none -> 11 us  [per_device(): jnp.concatenate(lax.all_to_all(jnp.stack(jnp.split(partial_value[None], l...]
where the time goes in v2:
time: 929 us; the launch traced here: 928 us
  waiting for transfers between devices  436 us (47%)
  blocking collectives  369 us (40%)
  local copies, waits for them, and re-layouts  62 us (7%)
  matrix products  18.9 us (2%)
  other arithmetic  17.8 us (2%)
  between operations  14.7 us (2%)
    all_to_all x1, blocking collectives, per_device(): lax.all_to_all(jnp.stack(jnp.split(partial_value[None], lax.axis_size('ro...  369 us
    all_to_all x1, waiting for transfers between devices, per_device(): lax.all_to_all(jnp.concatenate(lax.all_to_all(jnp.stack(jnp.split(partial...  362 us
    all_gather x1, waiting for transfers between devices, per_device(): lax.all_gather(int_masked, 'row', axis=2, tiled=True)  74.1 us
    unnamed x17, local copies, waits for them, and re-layouts  47.5 us
    dot_general x1, matrix products, per_device(): jnp.einsum('ikac,kjbc->ijab', amp_masked, lax.all_gather(int_masked, 'row...  18.9 us
  transfers between devices with their start and end apart: 2, of which 2 were waited for; matrix products, arithmetic and copies ran while one was open for 0% of the time, Pallas kernels for 0%

profile of v2, /device:TPU:1, one launch (start us, length us, event | category | flops | bytes accessed | tf_op | source)
XLA Modules:
  0.0 928.1 jit_solution(13373257223266775989)
XLA Ops:
  6.5 0.0 all-gather.2.cloned.1.call-start
  6.5 0.8 convert_bitcast_fusion
  7.3 0.1 broadcast_in_dim.6
  7.4 0.1 convert_element_type.63
  7.5 1.9 copy_multiply_fusion
  9.4 0.0 all-gather.2.cloned.1.call-update
  9.4 0.1 broadcast_in_dim.7
  9.4 0.1 convert_element_type.66
  9.5 74.1 %all-gather.2.cloned.1.call-done = bf16[4,8,1024,128]{3,2,0,1:T(8,128)(2,1)} async-done(((bf16[4,8,64,128]{3,2,0,1:T(8,128)(2,1)}), bf16[4,8,1024,128]{3,2,0,1:T(8,128)(2,1)}) %all-gather.2.cloned.1.call-update) | async-done | bytes 8388624 | tf_op jit(solution)/shard_map/all_gather | solution.py:37
  83.6 18.9 %convolution_bitcast_fusion = f32[1,16,8,64,1024]{4,3,1,2,0:T(8,128)} fusion(bf16[4,8,1024,128]{3,2,0,1:T(8,128)(2,1)} %all-gather.2.cloned.1.call-done, bf16[16,4,64,128]{3,2,1,0:T(8,128)(2,1)} %param.7, bf16[128]{0:T(256)(128)(2,1)S(1)} %convert_element_type.66), kind=kOutput, calls=%fused_computation | convolution fusion | flops 8592031744 | bytes 42991872 | tf_op jit(solution)/shard_map/ikac,kjbc->ijab/dot_general | solution.py:34
  102.5 3.2 fusion.17
  105.7 3.2 fusion.16
  108.9 3.2 fusion.15
  112.0 3.2 fusion.14
  115.2 3.2 fusion.13
  118.4 3.1 fusion.12
  121.5 3.2 fusion.11
  124.7 3.1 fusion.10
  127.8 3.2 fusion.9
  131.0 3.2 fusion.8
  134.2 3.1 fusion.7
  137.4 3.1 fusion.6
  140.5 3.2 fusion.5
  143.7 3.1 fusion.4
  146.8 3.2 fusion.3
  150.0 3.2 fusion.2
  153.2 369.4 %all_to_all.14 = f32[16,1,1,8,64,1024]{5,4,3,2,1,0:T(8,128)S(1)} all-to-all(f32[16,1,1,8,64,1024]{5,4,3,2,1,0:T(8,128)} %fusion.2), channel_id=1, replica_groups=mesh['row'=16,'col'=8] {'row'}, dimensions={0} | all-to-all | bytes 67108864 | tf_op jit(solution)/shard_map/all_to_all | solution.py:42
  522.6 11.0 %copy.57 = f32[1,1,8,16,64,1024]{5,4,3,2,1,0:T(8,128)} copy(f32[1,1,8,16,64,1024]{5,4,2,1,0,3:T(8,128)S(1)} %bitcast.125) | data formatting | bytes 67108864 | tf_op jit(solution)/shard_map/reshape | solution.py:41
  533.6 8.9 all-to-all-start.1
  542.6 0.0 copy-start
  543.9 362.2 %all-to-all-done.1 = f32[1,1,8,1024,1024]{4,3,1,0,2:T(8,128)} async-done(((f32[1,1,8,1024,1024]{4,3,1,0,2:T(8,128)}), f32[1,1,8,1024,1024]{4,3,1,0,2:T(8,128)}, u32[]{:S(2)}, u32[]{:S(2)}) %all-to-all-start.1) | async-done | bytes 33554464 | tf_op jit(solution)/shard_map/all_to_all | solution.py:40
  906.1 12.9 %reduce_sum.9 = bf16[1024,1024]{1,0:T(8,128)(2,1)S(1)} reduce(f32[1,1,8,1024,1024]{4,3,1,0,2:T(8,128)} %all-to-all-done.1, f32[]{:T(128)} %constant.16.clone.1), dimensions={0,1,2}, to_apply=%region_0.0 | reduce | flops 7340032 | bytes 35651588 | tf_op jit(solution)/shard_map/reduce_sum | solution.py:52
  919.0 0.0 copy-done
  919.0 2.3 fusion.1
Async XLA Ops:
  6.5 77.1 %all-gather.2.cloned.1.call-start = ((), (), s32[]{:S(2)}) async-start(), calls=%async_computation.2 | async-start | bytes 8912896 | tf_op jit(solution)/shard_map/all_gather | solution.py:37
  533.6 372.4 %all-to-all-start.1 = ((f32[1,1,8,1024,1024]{4,3,1,0,2:T(8,128)}), f32[1,1,8,1024,1024]{4,3,1,0,2:T(8,128)}, u32[]{:S(2)}, u32[]{:S(2)}) async-start(f32[1,1,8,1024,1024]{4,3,1,0,2:T(8,128)} %bitcast.124), calls=%async_computation.1 | async-start | bytes 67108864 | tf_op jit(solution)/shard_map/all_to_all | solution.py:40
  542.6 376.4 %copy-start = (f32[1024]{0:T(1024)S(1)}, f32[1024]{0:T(1024)}, u32[]{:S(2)}) copy-start(f32[1024]{0:T(1024)} %param.13) | copy-start | bytes 12292
Sparse Core Ops, SparseCore 0:
  9.5 74.0 all-gather.1
